TPU v7x, 32 devices: a whole 2x2x4 slice. The times are simulated.
32 devices in a mesh: prow: 4 (over x, core), pcol: 8 (over z, y).
Axes of the slice: x: 2, y: 2, z: 4, core: 2. Of those that a mesh axis runs over, the one named last changes fastest.
Arguments:
- b_leaf: bfloat16 [64, 256, 256], P('pcol', 'prow'), may hold values from -6 to 6
- dinv_leaf: bfloat16 [64, 256, 256], P('pcol'), as said below
- b_sep: bfloat16 [32, 256, 256], P('prow', 'pcol'), may hold values from -6 to 6
- dinv_sep: bfloat16 [32, 256, 256], P('prow'), as said below
- coupling: bfloat16 [32, 64, 256, 256], P('prow', 'pcol'), may hold values from -0.0625 to 0.0625
- pattern: int32 [32, 64], P('prow', 'pcol'), may hold values 0 or 1
Outputs:
- x_leaf: float32 [64, 256, 256], P('pcol', 'prow')
- x_sep: float32 [32, 256, 256], P('prow', 'pcol')
Inputs may be any that keep to these rules, and one draw needn't show every extreme that they name: pattern holds only 0 and 1. dinv_leaf is a full matrix for every supernode. dinv_sep is a full matrix for every supernode.
All inputs are finite; a program needn't handle non-finite values. No bound on the sum of `pattern` on one device may be relied on, other than what follows from the above.
Results may differ from a plain program's by a relative error of at most 0.0048.
Values may be sent and summed in bfloat16 or wider, within the bound.
A program may use at most 64 MiB of HBM per device.

v0:
```python
import jax
import jax.numpy as jnp
from jax import lax
from jax.sharding import PartitionSpec as P


def separator_values(reduced, dinv_sep):
    reduced_b = reduced.astype(jnp.bfloat16)
    forward_sep = jnp.einsum(
        "srk,sjk->srj", reduced_b, dinv_sep, preferred_element_type=jnp.float32
    ).astype(jnp.bfloat16)
    return jnp.einsum("srk,skj->srj", forward_sep, dinv_sep, preferred_element_type=jnp.float32)


def shards(b_leaf, dinv_leaf, b_sep, dinv_sep, coupling, pattern):
    masked = coupling * pattern.astype(coupling.dtype)[:, :, None, None]
    solved_share = jnp.einsum(
        "lrk,ljk->lrj", b_leaf, dinv_leaf, preferred_element_type=jnp.float32
    ).astype(jnp.bfloat16)
    solved = lax.all_gather(solved_share, "prow", axis=1, tiled=True)
    piece = solved
    partial_sums = lax.psum_scatter(
        jnp.einsum("lrk,sljk->rsj", piece, masked, preferred_element_type=jnp.float32),
        "pcol",
        scatter_dimension=0,
        tiled=True,
    )
    reduced = b_sep.astype(jnp.float32) - jnp.transpose(partial_sums, (1, 0, 2))
    x_sep = separator_values(reduced, dinv_sep)
    x_send = lax.all_gather(x_sep.astype(jnp.bfloat16), "pcol", axis=1, tiled=True)
    piece = x_send
    back_sums = lax.psum_scatter(
        jnp.einsum("srj,sljk->rlk", piece, masked, preferred_element_type=jnp.float32),
        "prow",
        scatter_dimension=0,
        tiled=True,
    )
    corrected = solved_share.astype(jnp.float32) - jnp.transpose(back_sums, (1, 0, 2))
    x_leaf = jnp.einsum(
        "lrk,lkj->lrj",
        corrected.astype(jnp.bfloat16),
        dinv_leaf,
        preferred_element_type=jnp.float32,
    )
    return (x_leaf, x_sep)


def solution(mesh):
    return jax.shard_map(
        shards,
        mesh=mesh,
        in_specs=(
            P("pcol", "prow", None),
            P("pcol", None, None),
            P("prow", "pcol", None),
            P("prow", None, None),
            P("prow", "pcol", None, None),
            P("prow", "pcol"),
        ),
        out_specs=(P("pcol", "prow", None), P("prow", "pcol", None)),
        check_vma=False,
    )
```

profile of v0, /device:TPU:0, one launch (start us, length us, event | category | flops | bytes accessed | tf_op | source)
XLA Modules:
  0.0 194.7 jit_solution(11816911248216911361)
XLA Ops:
  7.2 0.0 copy-start
  7.2 0.0 all-gather.3.cloned.1.call-start
  7.2 1.2 copy-done
  8.4 2.1 %convolution_convert_fusion = bf16[8,64,256]{2,1,0:T(8,128)(2,1)} fusion(bf16[8,64,256]{2,1,0:T(8,128)(2,1)} %param.6, bf16[8,256,256]{2,1,0:T(8,128)(2,1)S(1)} %copy-done), kind=kOutput, calls=%fused_computation.8 | convolution fusion | flops 67239936 | bytes 1572864 | tf_op jit(solution)/shard_map/lrk,ljk->lrj/dot_general | solution.py:17
  10.5 0.0 all-gather.3.cloned.1.call-update
  10.5 0.0 reduce-scatter.3.cloned.1.call-start
  10.6 0.7 convert_element_type.27
  11.3 0.0 copy-start.1
  11.3 0.0 copy-start.3
  11.3 18.8 %all-gather.3.cloned.1.call-done = bf16[8,256,256]{2,1,0:T(8,128)(2,1)} async-done(((bf16[8,64,256]{2,1,0:T(8,128)(2,1)}), bf16[8,256,256]{2,1,0:T(8,128)(2,1)}) %all-gather.3.cloned.1.call-update) | async-done | bytes 1048592 | tf_op jit(solution)/shard_map/all_gather | solution.py:20
  30.1 7.5 %fusion.6 = f32[256,8,256]{2,0,1:T(8,128)} fusion(bf16[8,8,256,256]{3,2,1,0:T(8,128)(2,1)} %param.10, bf16[8,8]{1,0:T(8,128)(2,1)S(1)} %convert_element_type.27, bf16[8,256,256]{2,1,0:T(8,128)(2,1)} %all-gather.3.cloned.1.call-done), kind=kOutput, calls=%fused_computation.6 | convolution fusion | flops 2164260864 | bytes 11534464 | tf_op jit(solution)/shard_map/lrk,sljk->rsj/dot_general | solution.py:23
  37.6 0.0 reduce-scatter.3.cloned.1.call-update
  37.6 0.0 all-gather.5.cloned.1.call-start
  37.7 69.2 %reduce-scatter.3.cloned.1.call-done = f32[32,8,256]{2,0,1:T(8,128)} async-done(((f32[256,8,256]{2,0,1:T(8,128)}), f32[32,8,256]{2,0,1:T(8,128)}) %reduce-scatter.3.cloned.1.call-update) | async-done | bytes 262160 | tf_op jit(solution)/shard_map/reduce_scatter | solution.py:22
  106.9 0.0 copy-done.1
  106.9 0.0 copy-done.3
  106.9 2.3 %fusion.21 = (bf16[8,32,256]{2,1,0:T(8,128)(2,1)}, f32[8,32,256]{2,1,0:T(8,128)}) fusion(bf16[8,256,256]{2,1,0:T(8,128)(2,1)S(1)} %copy-done.1, f32[32,8,256]{2,0,1:T(8,128)} %reduce-scatter.3.cloned.1.call-done, bf16[8,32,256]{2,1,0:T(8,128)(2,1)S(1)} %copy-done.3), kind=kOutput, calls=%fused_computation.18 | convolution fusion | flops 67436544 | bytes 1835008 | tf_op jit(solution)/shard_map/srk,skj->srj/dot_general | solution.py:12
  109.1 0.0 all-gather.5.cloned.1.call-update
  109.2 0.0 copy-start.2
  109.2 0.0 reduce-scatter.5.cloned.1.call-start
  109.2 39.3 %all-gather.5.cloned.1.call-done = bf16[8,256,256]{2,1,0:T(8,128)(2,1)} async-done(((bf16[8,32,256]{2,1,0:T(8,128)(2,1)}), bf16[8,256,256]{2,1,0:T(8,128)(2,1)}) %all-gather.5.cloned.1.call-update) | async-done | bytes 1048592 | tf_op jit(solution)/shard_map/all_gather | solution.py:30
  148.5 7.5 %fusion.9 = f32[256,8,256]{2,0,1:T(8,128)} fusion(bf16[8,8,256,256]{3,2,1,0:T(8,128)(2,1)} %param.10, bf16[8,8]{1,0:T(8,128)(2,1)S(1)} %convert_element_type.27, bf16[8,256,256]{2,1,0:T(8,128)(2,1)} %all-gather.5.cloned.1.call-done), kind=kOutput, calls=%fused_computation.7 | convolution fusion | flops 2164260864 | bytes 11534464 | tf_op jit(solution)/shard_map/srj,sljk->rlk/dot_general | solution.py:33
  156.0 0.0 reduce-scatter.5.cloned.1.call-update
  156.0 30.0 %reduce-scatter.5.cloned.1.call-done = f32[64,8,256]{2,0,1:T(8,128)} async-done(((f32[256,8,256]{2,0,1:T(8,128)}), f32[64,8,256]{2,0,1:T(8,128)}) %reduce-scatter.5.cloned.1.call-update) | async-done | bytes 524304 | tf_op jit(solution)/shard_map/reduce_scatter | solution.py:32
  186.0 0.0 copy-done.2
  186.0 2.1 %fusion.16 = f32[8,64,256]{2,1,0:T(8,128)} fusion(bf16[8,256,256]{2,1,0:T(8,128)(2,1)S(1)} %copy-done, f32[64,8,256]{2,0,1:T(8,128)} %reduce-scatter.5.cloned.1.call-done, bf16[8,64,256]{2,1,0:T(8,128)(2,1)S(1)} %copy-done.2), kind=kOutput, calls=%fused_computation.15 | convolution fusion | flops 67502080 | bytes 2359296 | tf_op jit(solution)/shard_map/lrk,lkj->lrj/dot_general | solution.py:39
Async XLA Ops:
  7.2 1.2 copy-start
  7.2 22.9 %all-gather.3.cloned.1.call-start = ((), (), s32[]{:S(2)}) async-start(), calls=%async_computation.2 | async-start | bytes 1310720 | tf_op jit(solution)/shard_map/all_gather | solution.py:20
  10.5 96.3 %reduce-scatter.3.cloned.1.call-start = ((), (), s32[]{:S(2)}) async-start(), calls=%async_computation.3 | async-start | bytes 2359296 | tf_op jit(solution)/shard_map/reduce_scatter | solution.py:22
  11.3 95.6 %copy-start.1 = (bf16[8,256,256]{2,1,0:T(8,128)(2,1)S(1)}, bf16[8,256,256]{2,1,0:T(8,128)(2,1)}, u32[]{:S(2)}) copy-start(bf16[8,256,256]{2,1,0:T(8,128)(2,1)} %param.9) | copy-start | bytes 3145732
  11.3 95.6 %copy-start.3 = (bf16[8,32,256]{2,1,0:T(8,128)(2,1)S(1)}, bf16[8,32,256]{2,1,0:T(8,128)(2,1)}, u32[]{:S(2)}) copy-start(bf16[8,32,256]{2,1,0:T(8,128)(2,1)} %param.8) | copy-start | bytes 393220
  37.6 110.9 %all-gather.5.cloned.1.call-start = ((), (), s32[]{:S(2)}) async-start(), calls=%async_computation.4 | async-start | bytes 1179648 | tf_op jit(solution)/shard_map/all_gather | solution.py:30
  109.2 76.8 %copy-start.2 = (bf16[8,64,256]{2,1,0:T(8,128)(2,1)S(1)}, bf16[8,64,256]{2,1,0:T(8,128)(2,1)}, u32[]{:S(2)}) copy-start(bf16[8,64,256]{2,1,0:T(8,128)(2,1)} %convolution_convert_fusion) | copy-start | bytes 786436
  109.2 76.8 %reduce-scatter.5.cloned.1.call-start = ((), (), s32[]{:S(2)}) async-start(), calls=%async_computation.5 | async-start | bytes 2621440 | tf_op jit(solution)/shard_map/reduce_scatter | solution.py:32
Sparse Core Ops, SparseCore 0:
  10.6 19.4 all-gather.2
  37.7 69.0 reduce-scatter.2
  109.3 39.1 all-gather.4
  156.1 29.8 reduce-scatter.4
where the time goes:
time: 195 us
  waiting for transfers between devices  157 us (81%)
  matrix products  21.5 us (11%)
  between operations  13.8 us (7%)
    reduce_scatter x1, waiting for transfers between devices, shards(): lax.psum_scatter(jnp.einsum('lrk,sljk->rsj', piece, masked, preferred_ele...  69.2 us
    all_gather x1, waiting for transfers between devices, shards(): lax.all_gather(x_sep.astype(jnp.bfloat16), 'pcol', axis=1, tiled=True)  39.3 us
    reduce_scatter x1, waiting for transfers between devices, shards(): lax.psum_scatter(jnp.einsum('srj,sljk->rlk', piece, masked, preferred_ele...  30 us
    all_gather x1, waiting for transfers between devices, shards(): solved = lax.all_gather(solved_share, 'prow', axis=1, tiled=True)  18.8 us
    dot_general x1, matrix products, shards(): jnp.einsum('lrk,sljk->rsj', piece, masked, preferred_element_type=jnp.flo...  7.49 us
    dot_general x1, matrix products, shards(): jnp.einsum('srj,sljk->rlk', piece, masked, preferred_element_type=jnp.flo...  7.48 us
  transfers between devices with their start and end apart: 4, of which 4 were waited for; matrix products, arithmetic and copies ran while one was open for 0% of the time, Pallas kernels for 0%

commit v1 on v0

v1 whole, which is shorter than its diff:
```python
import functools

import jax
import jax.numpy as jnp
from jax import lax
from jax.experimental import pallas as pl
from jax.experimental.pallas import tpu as pltpu
from jax.sharding import PartitionSpec as P

BF = jnp.bfloat16
F32 = jnp.float32
MESH = pl.DeviceIdType.MESH


def factors(pc):
    ny = 1
    while 2 * ny * ny <= pc // 2:
        ny *= 2
    return pc // ny, ny


def dot_t(a, b):
    return lax.dot_general(a, b, (((1,), (1,)), ((), ())), preferred_element_type=F32)


def dot_n(a, b):
    return lax.dot_general(a, b, (((1,), (0,)), ((), ())), preferred_element_type=F32)


def rows_of(v):
    n, r, w = v.shape
    if r % 16:
        return v.astype(F32).reshape(n * r, w).astype(v.dtype)
    return v.reshape(n * r, w)


def kernel(dims, b_leaf, dinv_leaf, b_sep, dinv_sep, coupling, pattern, x_leaf, x_sep,
           c_v, dl_v, ds_v, bs_v, bl_all, solved, pbuf, rec_y, zbuf, rec_z, xg, back,
           ebuf, rec_e1, e2buf, rec_e2, loc_sem, c_sem,
           a_s, a_r, as_s, as_r, y_s, y_r, z_s, z_r, d_s, d_r, f_s, f_r, e_s, e_r, g_s, g_r):
    nx, nz, ny, ls, ss, rl, rs, step = dims
    p, q = lax.axis_index("prow"), lax.axis_index("pcol")
    x, core = p // 2, p % 2
    z, y = q // ny, q % ny
    sib = (x * 2 + (1 - core), q)
    nch = ss // step
    lch = ls // step

    def at_x(d):
        return lax.rem(x + d + nx, nx)

    def at_y(d):
        return lax.rem(y + d + ny, ny)

    def at_z(d):
        return lax.rem(z + d + nz, nz)

    def dev_x(d):
        return (at_x(d) * 2 + core, q)

    def dev_y(d):
        return (p, z * ny + at_y(d))

    def dev_z(d):
        return (p, at_z(d) * ny + y)

    def remote(src, dst, s_sem, r_sem, dev):
        return pltpu.make_async_remote_copy(
            src_ref=src, dst_ref=dst, send_sem=s_sem, recv_sem=r_sem,
            device_id=dev, device_id_type=MESH)

    own = pltpu.make_async_copy(b_leaf, bl_all.at[p], loc_sem.at[0])
    own.start()
    locs = [pltpu.make_async_copy(dinv_leaf, dl_v, loc_sem.at[1]),
            pltpu.make_async_copy(dinv_sep, ds_v, loc_sem.at[2]),
            pltpu.make_async_copy(b_sep, bs_v, loc_sem.at[3])]
    cps = [pltpu.make_async_copy(coupling.at[s], c_v.at[s], c_sem.at[s]) for s in range(ss)]

    barrier = pltpu.get_barrier_semaphore()
    peers = ([dev_x(d) for d in range(1, nx)] + [sib] + [dev_y(d) for d in range(1, ny)]
             + [dev_z(d) for d in range(1, nz)])
    for dev in peers:
        pl.semaphore_signal(barrier, inc=1, device_id=dev, device_id_type=MESH)
    pl.semaphore_wait(barrier, len(peers))

    sends = []

    a_copies = {}
    as_copies = {}
    for t in range(lch):
        part = pl.ds(t * step, step)
        for d in range(1, nx):
            cp = remote(b_leaf.at[part], bl_all.at[p, part], a_s.at[d - 1, t], a_r.at[d - 1, t], dev_x(d))
            cp.start()
            a_copies[d, t] = cp
        cp = remote(b_leaf.at[part], bl_all.at[p, part], as_s.at[0, t], as_r.at[0, t], sib)
        cp.start()
        as_copies[0, t] = cp
    for cp in locs + cps:
        cp.start()

    def mask_row(s):
        cps[s].wait()

        @pl.loop(0, ls)
        def _(l):
            c_v[s, l] = c_v[s, l] * pattern[s, l].astype(F32).astype(BF)

    def forward_a(t):
        part = pl.ds(t * step, step)
        for d in range(1, nx):
            a_copies[d, t].wait_recv()
            src = bl_all.at[at_x(-d) * 2 + core, part]
            cp = remote(src, src, as_s.at[d, t], as_r.at[d, t], sib)
            cp.start()
            as_copies[d, t] = cp

    def solve_leaf(t):
        for d in range(nx):
            as_copies[d, t].wait_recv()

        @pl.loop(t * step, (t + 1) * step)
        def _(l):
            solved[l] = dot_t(rows_of(bl_all[:, l]), dl_v[l]).astype(BF)

    per = ss // lch
    for t in range(lch):
        for s in range(t * per, (t + 1) * per):
            mask_row(s)
        forward_a(t)
    own.wait()
    locs[0].wait()
    for t in range(lch):
        solve_leaf(t)
    locs[1].wait()
    locs[2].wait()

    y_copies, z_copies, d_copies, f_copies = {}, {}, {}, {}

    def partial(t):
        @pl.loop(t * step, (t + 1) * step)
        def _(s):
            total = dot_t(solved[0], c_v[s, 0])
            for l in range(1, ls):
                total += dot_t(solved[l], c_v[s, l])
            total = total.reshape(nz, ny, rs, total.shape[-1])
            for j in range(ny):
                pbuf[j, s] = total[:, j].astype(BF)
        part = pl.ds(t * step, step)
        for d in range(1, ny):
            cp = remote(pbuf.at[at_y(d), part], rec_y.at[d - 1, part],
                        y_s.at[d - 1, t], y_r.at[d - 1, t], dev_y(d))
            cp.start()
            y_copies[d, t] = cp

    def sum_y(t):
        for d in range(1, ny):
            y_copies[d, t].wait_recv()

        @pl.loop(t * step, (t + 1) * step)
        def _(s):
            total = pbuf[y, s].astype(F32)
            for d in range(1, ny):
                total += rec_y[d - 1, s].astype(F32)
            total = total.astype(BF)
            for j in range(nz):
                zbuf[j, s] = total[j]
        part = pl.ds(t * step, step)
        for d in range(1, nz):
            cp = remote(zbuf.at[at_z(d), part], rec_z.at[d - 1, part],
                        z_s.at[d - 1, t], z_r.at[d - 1, t], dev_z(d))
            cp.start()
            z_copies[d, t] = cp

    def solve_sep(t):
        for d in range(1, nz):
            z_copies[d, t].wait_recv()

        @pl.loop(t * step, (t + 1) * step)
        def _(s):
            total = zbuf[z, s].astype(F32)
            for d in range(1, nz):
                total += rec_z[d - 1, s].astype(F32)
            reduced = (bs_v[s].astype(F32) - total).astype(BF)
            fwd = dot_t(reduced, ds_v[s]).astype(BF)
            sol = dot_n(fwd, ds_v[s])
            x_sep[s] = sol
            xg[q, s] = sol.astype(BF)
        part = pl.ds(t * step, step)
        src = xg.at[q, part]
        for d in range(1, nz):
            cp = remote(src, src, d_s.at[d - 1, t], d_r.at[d - 1, t], dev_z(d))
            cp.start()
            d_copies[d, t] = cp
        for d in range(1, ny):
            cp = remote(src, src, f_s.at[d - 1, 0, t], f_r.at[d - 1, 0, t], dev_y(d))
            cp.start()
            f_copies[d, 0, t] = cp

    def forward_d(t):
        part = pl.ds(t * step, step)
        for e in range(1, nz):
            d_copies[e, t].wait_recv()
            src = xg.at[at_z(-e) * ny + y, part]
            for d in range(1, ny):
                cp = remote(src, src, f_s.at[d - 1, e, t], f_r.at[d - 1, e, t], dev_y(d))
                cp.start()
                f_copies[d, e, t] = cp

    def back_mm(t):
        for e in range(nz):
            for d in range(1, ny):
                f_copies[d, e, t].wait_recv()
        vals = [rows_of(xg[:, t * step + i]) for i in range(step)]

        @pl.loop(0, ls)
        def _(l):
            total = dot_n(vals[0], c_v[t * step, l])
            for i in range(1, step):
                total += dot_n(vals[i], c_v[t * step + i, l])
            if t == 0:
                back[l] = total
            else:
                back[l] += total

    stages = [(partial, 0), (sum_y, 2), (solve_sep, 4), (forward_d, 6), (back_mm, 8)]
    for i in range(nch + 9):
        for fn, lag in reversed(stages):
            if 0 <= i - lag < nch:
                fn(i - lag)

    e_copies, g_copies = {}, {}

    def split_e(t):
        @pl.loop(t * step, (t + 1) * step)
        def _(l):
            v = back[l].reshape(nx, 2, rl, back.shape[-1])
            ebuf[0, l] = v[:, 0].astype(BF)
            ebuf[1, l] = v[:, 1].astype(BF)
        part = pl.ds(t * step, step)
        cp = remote(ebuf.at[1 - core, part], rec_e1.at[part], e_s.at[t], e_r.at[t], sib)
        cp.start()
        e_copies[t] = cp

    def sum_e(t):
        e_copies[t].wait_recv()

        @pl.loop(t * step, (t + 1) * step)
        def _(l):
            total = (ebuf[core, l].astype(F32) + rec_e1[l].astype(F32)).astype(BF)
            for j in range(nx):
                e2buf[j, l] = total[j]
        part = pl.ds(t * step, step)
        for d in range(1, nx):
            cp = remote(e2buf.at[at_x(d), part], rec_e2.at[d - 1, part],
                        g_s.at[d - 1, t], g_r.at[d - 1, t], dev_x(d))
            cp.start()
            g_copies[d, t] = cp

    def final(t):
        for d in range(1, nx):
            g_copies[d, t].wait_recv()

        @pl.loop(t * step, (t + 1) * step)
        def _(l):
            total = e2buf[x, l].astype(F32)
            for d in range(1, nx):
                total += rec_e2[d - 1, l].astype(F32)
            mine = solved[l, pl.ds(pl.multiple_of(p * rl, rl), rl), :].astype(F32)
            x_leaf[l] = dot_n((mine - total).astype(BF), dl_v[l])

    for fn in (split_e, sum_e, final):
        for t in range(lch):
            fn(t)

    for group in (a_copies, as_copies, y_copies, z_copies, d_copies, f_copies, e_copies, g_copies):
        for cp in group.values():
            cp.wait_send()


def shards(pr, pc, b_leaf, dinv_leaf, b_sep, dinv_sep, coupling, pattern):
    nx = pr // 2
    nz, ny = factors(pc)
    ss, ls, bs, _ = coupling.shape
    rl, rs = b_leaf.shape[1], b_sep.shape[1]
    step = 2
    nch, lch = ss // step, ls // step
    any_, vmem = pl.BlockSpec(memory_space=pl.ANY), pl.BlockSpec(memory_space=pltpu.VMEM)
    dma = pltpu.SemaphoreType.DMA
    mx, my, mz = max(nx - 1, 1), max(ny - 1, 1), max(nz - 1, 1)
    sems = []
    for shape in ((mx, lch), (nx, lch), (my, nch), (mz, nch), (mz, nch), (my, nz, nch), (lch,), (mx, lch)):
        sems += [dma(shape), dma(shape)]
    return pl.pallas_call(
        functools.partial(kernel, (nx, nz, ny, ls, ss, rl, rs, step)),
        out_shape=(jax.ShapeDtypeStruct(b_leaf.shape, F32), jax.ShapeDtypeStruct(b_sep.shape, F32)),
        in_specs=[any_] * 5 + [pl.BlockSpec(memory_space=pltpu.SMEM)],
        out_specs=(vmem, vmem),
        scratch_shapes=[
            pltpu.VMEM(coupling.shape, BF),
            pltpu.VMEM(dinv_leaf.shape, BF),
            pltpu.VMEM(dinv_sep.shape, BF),
            pltpu.VMEM(b_sep.shape, BF),
            pltpu.VMEM((pr, ls, rl, bs), BF),
            pltpu.VMEM((ls, pr * rl, bs), BF),
            pltpu.VMEM((ny, ss, nz, rs, bs), BF),
            pltpu.VMEM((my, ss, nz, rs, bs), BF),
            pltpu.VMEM((nz, ss, rs, bs), BF),
            pltpu.VMEM((mz, ss, rs, bs), BF),
            pltpu.VMEM((pc, ss, rs, bs), BF),
            pltpu.VMEM((ls, pr * rl, bs), F32),
            pltpu.VMEM((2, ls, nx, rl, bs), BF),
            pltpu.VMEM((ls, nx, rl, bs), BF),
            pltpu.VMEM((nx, ls, rl, bs), BF),
            pltpu.VMEM((mx, ls, rl, bs), BF),
            dma((4,)), dma((ss,)),
        ] + sems,
        compiler_params=pltpu.CompilerParams(
            collective_id=0, has_side_effects=True, vmem_limit_bytes=50 * 1024 * 1024),
    )(b_leaf, dinv_leaf, b_sep, dinv_sep, coupling, pattern)


def solution(mesh):
    pr, pc = mesh.shape["prow"], mesh.shape["pcol"]
    return jax.shard_map(
        functools.partial(shards, pr, pc),
        mesh=mesh,
        in_specs=(
            P("pcol", "prow", None),
            P("pcol", None, None),
            P("prow", "pcol", None),
            P("prow", None, None),
            P("prow", "pcol", None, None),
            P("prow", "pcol"),
        ),
        out_specs=(P("pcol", "prow", None), P("prow", "pcol", None)),
        check_vma=False,
    )
```

time: 195 us -> 68 us (0.35)
  waiting for transfers between devices: 157 us -> 0 us
  Pallas kernels: 0 us -> 60.6 us
  matrix products: 21.5 us -> 0 us
  between operations: 13.8 us -> 0.65 us
  local copies, waits for them, and re-layouts: 1.19 us -> 6.48 us
    reduce_scatter x2 -> x0, waiting for transfers between devices: 99.2 us -> none  [the longest x1 69.2 us: shards(): lax.psum_scatter(jnp.einsum('lrk,sljk->rsj', piece, masked, preferred_ele...]
    pallas_call x0 -> x1, Pallas kernels: none -> 60.6 us  [shards(): pl.pallas_call(functools.partial(kernel, (nx, nz, ny, ls, ss, rl, rs, ste...]
    all_gather x2 -> x0, waiting for transfers between devices: 58.1 us -> none  [the longest x1 39.3 us: shards(): lax.all_gather(x_sep.astype(jnp.bfloat16), 'pcol', axis=1, tiled=True)]
    dot_general x5 -> x0, matrix products: 21.5 us -> none  [the longest x1 7.49 us: shards(): jnp.einsum('lrk,sljk->rsj', piece, masked, preferred_element_type=jnp.flo...]
    unnamed x8 -> x12, local copies, waits for them, and re-layouts: 1.19 us -> 6.48 us
  transfers between devices with their start and end apart: 4 -> 0, of which waited for: 4 -> 0; matrix products, arithmetic and copies ran while one was open for 0% -> 0% of each run, Pallas kernels for 0% -> 0%
where the time goes in v1:
time: 68 us; the launch traced here: 67.7 us
  Pallas kernels  60.6 us (89%)
  local copies, waits for them, and re-layouts  6.48 us (10%)
    pallas_call x1, Pallas kernels, shards(): pl.pallas_call(functools.partial(kernel, (nx, nz, ny, ls, ss, rl, rs, ste...  60.6 us
    unnamed x12, local copies, waits for them, and re-layouts  6.48 us

profile of v1, /device:TPU:0, one launch (start us, length us, event | category | flops | bytes accessed | tf_op | source)
XLA Modules:
  0.0 67.7 jit_solution(12127827655902028956)
XLA Ops:
  0.6 0.0 copy-start
  0.6 1.2 %copy-done = bf16[8,256,256]{2,1,0:T(8,128)(2,1)S(1)} copy-done((bf16[8,256,256]{2,1,0:T(8,128)(2,1)S(1)}, bf16[8,256,256]{2,1,0:T(8,128)(2,1)}, u32[]{:S(2)}) %copy-start) | copy-done | bytes 1048600
  1.9 0.0 copy-start.1
  1.9 1.2 %copy-done.1 = bf16[8,256,256]{2,1,0:T(8,128)(2,1)S(1)} copy-done((bf16[8,256,256]{2,1,0:T(8,128)(2,1)S(1)}, bf16[8,256,256]{2,1,0:T(8,128)(2,1)}, u32[]{:S(2)}) %copy-start.1) | copy-done | bytes 1048600
  3.1 0.0 copy-start.2
  3.1 0.9 %copy-done.2 = bf16[8,64,256]{2,1,0:T(8,128)(2,1)S(1)} copy-done((bf16[8,64,256]{2,1,0:T(8,128)(2,1)S(1)}, bf16[8,64,256]{2,1,0:T(8,128)(2,1)}, u32[]{:S(2)}) %copy-start.2) | copy-done | bytes 262168
  4.0 0.0 copy-start.3
  4.0 0.9 %copy-done.3 = bf16[8,32,256]{2,1,0:T(8,128)(2,1)S(1)} copy-done((bf16[8,32,256]{2,1,0:T(8,128)(2,1)S(1)}, bf16[8,32,256]{2,1,0:T(8,128)(2,1)}, u32[]{:S(2)}) %copy-start.3) | copy-done | bytes 131096
  4.9 0.0 copy-start.4
  4.9 0.7 %copy-done.4 = s32[8,8]{1,0:T(8,128)S(1)} copy-done((s32[8,8]{1,0:T(8,128)S(1)}, s32[8,8]{1,0:T(8,128)}, u32[]{:S(2)}) %copy-start.4) | copy-done | bytes 280
  5.6 60.6 %shard_map.77 = (f32[8,64,256]{2,1,0:T(8,128)S(1)}, f32[8,32,256]{2,1,0:T(8,128)S(1)}) custom-call(bf16[8,64,256]{2,1,0:T(8,128)(2,1)S(1)} %copy-done.2, bf16[8,256,256]{2,1,0:T(8,128)(2,1)S(1)} %copy-done, bf16[8,32,256]{2,1,0:T(8,128)(2,1)S(1)} %copy-done.3, bf16[8,256,256]{2,1,0:T(8,128)(2,1)S(1)} %copy-done.1, bf16[8,8,256,256]{3,2,1,0:T(8,128)(2,1)} %coupling.1, ...), custom_call_target="tpu_custom_call" | custom-call | tf_op jit(solution)/shard_map/pallas_call | solution.py:294
  66.2 0.8 %copy.10 = f32[8,64,256]{2,1,0:T(8,128)} copy(f32[8,64,256]{2,1,0:T(8,128)S(1)} %get-tuple-element.4) | data formatting | bytes 1048576
  67.0 0.7 %copy.11 = f32[8,32,256]{2,1,0:T(8,128)} copy(f32[8,32,256]{2,1,0:T(8,128)S(1)} %get-tuple-element.5) | data formatting | bytes 524288
Async XLA Ops:
  0.6 1.2 %copy-start = (bf16[8,256,256]{2,1,0:T(8,128)(2,1)S(1)}, bf16[8,256,256]{2,1,0:T(8,128)(2,1)}, u32[]{:S(2)}) copy-start(bf16[8,256,256]{2,1,0:T(8,128)(2,1)} %dinv_leaf.1) | copy-start | bytes 3145732
  1.9 1.2 %copy-start.1 = (bf16[8,256,256]{2,1,0:T(8,128)(2,1)S(1)}, bf16[8,256,256]{2,1,0:T(8,128)(2,1)}, u32[]{:S(2)}) copy-start(bf16[8,256,256]{2,1,0:T(8,128)(2,1)} %dinv_sep.1) | copy-start | bytes 3145732
  3.1 0.9 %copy-start.2 = (bf16[8,64,256]{2,1,0:T(8,128)(2,1)S(1)}, bf16[8,64,256]{2,1,0:T(8,128)(2,1)}, u32[]{:S(2)}) copy-start(bf16[8,64,256]{2,1,0:T(8,128)(2,1)} %b_leaf.1) | copy-start | bytes 786436
  4.0 0.9 %copy-start.3 = (bf16[8,32,256]{2,1,0:T(8,128)(2,1)S(1)}, bf16[8,32,256]{2,1,0:T(8,128)(2,1)}, u32[]{:S(2)}) copy-start(bf16[8,32,256]{2,1,0:T(8,128)(2,1)} %b_sep.1) | copy-start | bytes 393220
  4.9 0.7 %copy-start.4 = (s32[8,8]{1,0:T(8,128)S(1)}, s32[8,8]{1,0:T(8,128)}, u32[]{:S(2)}) copy-start(s32[8,8]{1,0:T(8,128)} %pattern.1) | copy-start | bytes 772

commit v2 on v1

v2 whole, which is shorter than its diff:
```python
import functools

import jax
import jax.numpy as jnp
from jax import lax
from jax.experimental import pallas as pl
from jax.experimental.pallas import tpu as pltpu
from jax.sharding import PartitionSpec as P

BF = jnp.bfloat16
F32 = jnp.float32
MESH = pl.DeviceIdType.MESH
LAGS = (2, 5, 8, 10)


def factors(pc):
    ny = 1
    while 2 * ny * ny <= pc // 2:
        ny *= 2
    return pc // ny, ny


def dot_t(a, b):
    return lax.dot_general(a, b, (((1,), (1,)), ((), ())), preferred_element_type=F32)


def dot_n(a, b):
    return lax.dot_general(a, b, (((1,), (0,)), ((), ())), preferred_element_type=F32)


def rows_of(v):
    r, w = v.shape[-2:]
    if r % 16:
        return v.astype(F32).reshape(-1, w).astype(v.dtype)
    return v.reshape(-1, w)


def kernel(dims, b_leaf, dinv_leaf, b_sep, dinv_sep, coupling, pattern, x_leaf, x_sep,
           c_v, dl_v, ds_v, bs_v, bl_all, solved, pbuf, rec_y, zbuf, rec_z, xg, back,
           ebuf, rec_e1, e2buf, rec_e2, own_sem, loc_sem, c_sem,
           a_s, a_r, as_s, as_r, y_s, y_r, z_s, z_r, d_s, d_r, f_s, f_r, e_s, e_r, g_s, g_r):
    nx, nz, ny, ls, ss, g, nh, rs, step = dims
    rl = g * rs
    p, q = lax.axis_index("prow"), lax.axis_index("pcol")
    x, core = p // 2, p % 2
    z, y = q // ny, q % ny
    sib = (x * 2 + (1 - core), q)
    nch = ss // step
    lch = ls // step

    def at_x(d):
        return lax.rem(x + d + nx, nx)

    def at_y(d):
        return lax.rem(y + d + ny, ny)

    def at_z(d):
        return lax.rem(z + d + nz, nz)

    def dev_x(d):
        return (at_x(d) * 2 + core, q)

    def dev_y(d):
        return (p, z * ny + at_y(d))

    def dev_z(d):
        return (p, at_z(d) * ny + y)

    def remote(src, dst, s_sem, r_sem, dev):
        return pltpu.make_async_remote_copy(
            src_ref=src, dst_ref=dst, send_sem=s_sem, recv_sem=r_sem,
            device_id=dev, device_id_type=MESH)

    own = [pltpu.make_async_copy(b_leaf.at[:, :, h], bl_all.at[h, p], own_sem.at[h]) for h in range(nh)]
    for cp in own:
        cp.start()
    locs = [pltpu.make_async_copy(dinv_leaf, dl_v, loc_sem.at[1]),
            pltpu.make_async_copy(dinv_sep, ds_v, loc_sem.at[2]),
            pltpu.make_async_copy(b_sep, bs_v, loc_sem.at[3])]
    cps = [pltpu.make_async_copy(coupling.at[s], c_v.at[s], c_sem.at[s]) for s in range(ss)]

    barrier = pltpu.get_barrier_semaphore()
    peers = ([dev_x(d) for d in range(1, nx)] + [sib] + [dev_y(d) for d in range(1, ny)]
             + [dev_z(d) for d in range(1, nz)])
    for dev in peers:
        pl.semaphore_signal(barrier, inc=1, device_id=dev, device_id_type=MESH)
    pl.semaphore_wait(barrier, len(peers))

    a_copies = {}
    as_copies = {}
    for h in range(nh):
        for t in range(lch):
            u = h * lch + t
            part = pl.ds(t * step, step)
            for d in range(1, nx):
                cp = remote(b_leaf.at[part, :, h], bl_all.at[h, p, part], a_s.at[d - 1, u], a_r.at[d - 1, u], dev_x(d))
                cp.start()
                a_copies[d, u] = cp
            cp = remote(b_leaf.at[part, :, h], bl_all.at[h, p, part], as_s.at[0, u], as_r.at[0, u], sib)
            cp.start()
            as_copies[0, u] = cp
    for cp in locs + cps:
        cp.start()

    def mask_row(s):
        cps[s].wait()

        @pl.loop(0, ls)
        def _(l):
            c_v[s, l] = c_v[s, l] * pattern[s, l].astype(F32).astype(BF)

    def forward_a(u):
        h, part = u // lch, pl.ds(u % lch * step, step)
        for d in range(1, nx):
            a_copies[d, u].wait_recv()
            src = bl_all.at[h, at_x(-d) * 2 + core, part]
            cp = remote(src, src, as_s.at[d, u], as_r.at[d, u], sib)
            cp.start()
            as_copies[d, u] = cp

    def solve_leaf(u):
        h, t = u // lch, u % lch
        for d in range(nx):
            as_copies[d, u].wait_recv()

        @pl.loop(t * step, (t + 1) * step)
        def _(l):
            solved[h, l] = dot_t(rows_of(bl_all[h, :, l]), dl_v[l]).astype(BF)

    y_copies, z_copies, d_copies, f_copies = {}, {}, {}, {}

    def partial(u):
        h, t = u // nch, u % nch

        @pl.loop(t * step, (t + 1) * step)
        def _(s):
            total = dot_t(solved[h, 0], c_v[s, 0])
            for l in range(1, ls):
                total += dot_t(solved[h, l], c_v[s, l])
            total = total.reshape(nz, ny, rs, total.shape[-1])
            for j in range(ny):
                pbuf[h, j, s] = total[:, j].astype(BF)
        part = pl.ds(t * step, step)
        for d in range(1, ny):
            cp = remote(pbuf.at[h, at_y(d), part], rec_y.at[h, d - 1, part],
                        y_s.at[d - 1, u], y_r.at[d - 1, u], dev_y(d))
            cp.start()
            y_copies[d, u] = cp

    def sum_y(u):
        h, t = u // nch, u % nch
        for d in range(1, ny):
            y_copies[d, u].wait_recv()

        @pl.loop(t * step, (t + 1) * step)
        def _(s):
            total = pbuf[h, y, s].astype(F32)
            for d in range(1, ny):
                total += rec_y[h, d - 1, s].astype(F32)
            total = total.astype(BF)
            for j in range(nz):
                zbuf[h, j, s] = total[j]
        part = pl.ds(t * step, step)
        for d in range(1, nz):
            cp = remote(zbuf.at[h, at_z(d), part], rec_z.at[h, d - 1, part],
                        z_s.at[d - 1, u], z_r.at[d - 1, u], dev_z(d))
            cp.start()
            z_copies[d, u] = cp

    def solve_sep(u):
        h, t = u // nch, u % nch
        for d in range(1, nz):
            z_copies[d, u].wait_recv()

        @pl.loop(t * step, (t + 1) * step)
        def _(s):
            total = zbuf[h, z, s].astype(F32)
            for d in range(1, nz):
                total += rec_z[h, d - 1, s].astype(F32)
            reduced = (bs_v[s, h].astype(F32) - total).astype(BF)
            fwd = dot_t(reduced, ds_v[s]).astype(BF)
            sol = dot_n(fwd, ds_v[s])
            x_sep[s, h] = sol
            xg[h, q, s] = sol.astype(BF)
        src = xg.at[h, q, pl.ds(t * step, step)]
        for d in range(1, nz):
            cp = remote(src, src, d_s.at[d - 1, u], d_r.at[d - 1, u], dev_z(d))
            cp.start()
            d_copies[d, u] = cp
        for d in range(1, ny):
            cp = remote(src, src, f_s.at[d - 1, 0, u], f_r.at[d - 1, 0, u], dev_y(d))
            cp.start()
            f_copies[d, 0, u] = cp

    def forward_d(u):
        h, part = u // nch, pl.ds(u % nch * step, step)
        for e in range(1, nz):
            d_copies[e, u].wait_recv()
            src = xg.at[h, at_z(-e) * ny + y, part]
            for d in range(1, ny):
                cp = remote(src, src, f_s.at[d - 1, e, u], f_r.at[d - 1, e, u], dev_y(d))
                cp.start()
                f_copies[d, e, u] = cp

    def back_mm(u):
        h, t = u // nch, u % nch
        for e in range(nz):
            for d in range(1, ny):
                f_copies[d, e, u].wait_recv()
        vals = [rows_of(xg[h, :, t * step + i]) for i in range(step)]

        @pl.loop(0, ls)
        def _(l):
            total = dot_n(vals[0], c_v[t * step, l])
            for i in range(1, step):
                total += dot_n(vals[i], c_v[t * step + i, l])
            if t == 0:
                back[h, l] = total
            else:
                back[h, l] += total

    e_copies, g_copies = {}, {}

    def split_e(u):
        h, t = u // lch, u % lch

        @pl.loop(t * step, (t + 1) * step)
        def _(l):
            v = back[h, l].reshape(nx, 2, rl, back.shape[-1])
            ebuf[h, 0, l] = v[:, 0].astype(BF)
            ebuf[h, 1, l] = v[:, 1].astype(BF)
        part = pl.ds(t * step, step)
        cp = remote(ebuf.at[h, 1 - core, part], rec_e1.at[h, part], e_s.at[u], e_r.at[u], sib)
        cp.start()
        e_copies[u] = cp

    def sum_e(u):
        h, t = u // lch, u % lch
        e_copies[u].wait_recv()

        @pl.loop(t * step, (t + 1) * step)
        def _(l):
            total = (ebuf[h, core, l].astype(F32) + rec_e1[h, l].astype(F32)).astype(BF)
            for j in range(nx):
                e2buf[h, j, l] = total[j]
        part = pl.ds(t * step, step)
        for d in range(1, nx):
            cp = remote(e2buf.at[h, at_x(d), part], rec_e2.at[h, d - 1, part],
                        g_s.at[d - 1, u], g_r.at[d - 1, u], dev_x(d))
            cp.start()
            g_copies[d, u] = cp

    def final(u):
        h, t = u // lch, u % lch
        for d in range(1, nx):
            g_copies[d, u].wait_recv()

        @pl.loop(t * step, (t + 1) * step)
        def _(l):
            total = e2buf[h, x, l].astype(F32)
            for d in range(1, nx):
                total += rec_e2[h, d - 1, l].astype(F32)
            mine = solved[h, l, pl.ds(pl.multiple_of(p * rl, rl), rl), :].astype(F32)
            sol = dot_n((mine - total).astype(BF), dl_v[l])
            x_leaf[l, :, h] = sol.reshape(g, rs, sol.shape[-1])

    per = ss // lch
    tasks = []
    for t in range(lch):
        tasks += [(mask_row, s) for s in range(t * per, (t + 1) * per)] + [(forward_a, t)]
    tasks += [(solve_leaf, t) for t in range(lch)]
    stages = [(partial, 0), (sum_y, LAGS[0]), (solve_sep, LAGS[1]), (forward_d, LAGS[2]), (back_mm, LAGS[3])]
    total_u = nh * nch
    for i in range(total_u + LAGS[3]):
        for fn, lag in reversed(stages):
            u = i - lag
            if not 0 <= u < total_u:
                continue
            h, t = u // nch, u % nch
            if fn is partial and t == 0 and h > 0:
                tasks += [(solve_leaf, h * lch + k) for k in range(lch)]
            tasks.append((fn, u))
            if fn is partial and t == nch // 2 and h + 1 < nh:
                tasks += [(forward_a, (h + 1) * lch + k) for k in range(lch)]
            if fn is back_mm:
                if h > 0 and t == nch // 2 - 1:
                    tasks += [(sum_e, (h - 1) * lch + k) for k in range(lch)]
                if t == nch - 1:
                    tasks += [(split_e, h * lch + k) for k in range(lch)]
                    if h > 0:
                        tasks += [(final, (h - 1) * lch + k) for k in range(lch)]
    tasks += [(fn, (nh - 1) * lch + k) for fn in (sum_e, final) for k in range(lch)]

    for k, (fn, u) in enumerate(tasks):
        if fn is solve_leaf and u % lch == 0:
            own[u // lch].wait()
            if u == 0:
                locs[0].wait()
        if fn is solve_sep and u == 0:
            locs[1].wait()
            locs[2].wait()
        fn(u)

    for group in (a_copies, as_copies, y_copies, z_copies, d_copies, f_copies, e_copies, g_copies):
        for cp in group.values():
            cp.wait_send()


def shards(pr, pc, b_leaf, dinv_leaf, b_sep, dinv_sep, coupling, pattern):
    nx = pr // 2
    nz, ny = factors(pc)
    ss, ls, bs, _ = coupling.shape
    g = pc // pr
    nh = 2 if b_sep.shape[1] >= 16 else 1
    rs = b_sep.shape[1] // nh
    rl = g * rs
    step = 2
    nch, lch = ss // step, ls // step
    nu, lu = nh * nch, nh * lch
    hbm, vmem = pl.BlockSpec(memory_space=pltpu.HBM), pl.BlockSpec(memory_space=pltpu.VMEM)
    dma = pltpu.SemaphoreType.DMA
    mx, my, mz = max(nx - 1, 1), max(ny - 1, 1), max(nz - 1, 1)
    sems = []
    for shape in ((mx, lu), (nx, lu), (my, nu), (mz, nu), (mz, nu), (my, nz, nu), (lu,), (mx, lu)):
        sems += [dma(shape), dma(shape)]
    x_leaf, x_sep = pl.pallas_call(
        functools.partial(kernel, (nx, nz, ny, ls, ss, g, nh, rs, step)),
        out_shape=(jax.ShapeDtypeStruct((ls, g, nh, rs, bs), F32), jax.ShapeDtypeStruct((ss, nh, rs, bs), F32)),
        in_specs=[hbm] * 5 + [pl.BlockSpec(memory_space=pltpu.SMEM)],
        out_specs=(vmem, vmem),
        scratch_shapes=[
            pltpu.VMEM(coupling.shape, BF),
            pltpu.VMEM(dinv_leaf.shape, BF),
            pltpu.VMEM(dinv_sep.shape, BF),
            pltpu.VMEM((ss, nh, rs, bs), BF),
            pltpu.VMEM((nh, pr, ls, g, rs, bs), BF),
            pltpu.VMEM((nh, ls, pr * rl, bs), BF),
            pltpu.VMEM((nh, ny, ss, nz, rs, bs), BF),
            pltpu.VMEM((nh, my, ss, nz, rs, bs), BF),
            pltpu.VMEM((nh, nz, ss, rs, bs), BF),
            pltpu.VMEM((nh, mz, ss, rs, bs), BF),
            pltpu.VMEM((nh, pc, ss, rs, bs), BF),
            pltpu.VMEM((nh, ls, pr * rl, bs), F32),
            pltpu.VMEM((nh, 2, ls, nx, rl, bs), BF),
            pltpu.VMEM((nh, ls, nx, rl, bs), BF),
            pltpu.VMEM((nh, nx, ls, rl, bs), BF),
            pltpu.VMEM((nh, mx, ls, rl, bs), BF),
            dma((nh,)), dma((4,)), dma((ss,)),
        ] + sems,
        compiler_params=pltpu.CompilerParams(
            collective_id=0, has_side_effects=True, vmem_limit_bytes=67043328),
    )(b_leaf.reshape(ls, g, nh, rs, bs), dinv_leaf, b_sep.reshape(ss, nh, rs, bs), dinv_sep, coupling, pattern)
    return x_leaf.reshape(b_leaf.shape), x_sep.reshape(b_sep.shape)


def solution(mesh):
    pr, pc = mesh.shape["prow"], mesh.shape["pcol"]
    return jax.shard_map(
        functools.partial(shards, pr, pc),
        mesh=mesh,
        in_specs=(
            P("pcol", "prow", None),
            P("pcol", None, None),
            P("prow", "pcol", None),
            P("prow", None, None),
            P("prow", "pcol", None, None),
            P("prow", "pcol"),
        ),
        out_specs=(P("pcol", "prow", None), P("prow", "pcol", None)),
        check_vma=False,
    )
```

time: 68 us -> 68.8 us (1.012)
  Pallas kernels: 60.6 us -> 64.4 us
  local copies, waits for them, and re-layouts: 6.48 us -> 3.54 us
    pallas_call x1, Pallas kernels: 60.6 us -> 64.4 us  [shards(): pl.pallas_call(functools.partial(kernel, (nx, nz, ny, ls, ss, g, nh, rs,...]
    unnamed x12 -> x2, local copies, waits for them, and re-layouts: 6.48 us -> 3.54 us
where the time goes in v2:
time: 68.8 us; the launch traced here: 68.6 us
  Pallas kernels  64.4 us (94%)
  local copies, waits for them, and re-layouts  3.54 us (5%)
    pallas_call x1, Pallas kernels, shards(): pl.pallas_call(functools.partial(kernel, (nx, nz, ny, ls, ss, g, nh, rs,...  64.4 us
    unnamed x2, local copies, waits for them, and re-layouts  3.54 us

profile of v2, /device:TPU:0, one launch (start us, length us, event | category | flops | bytes accessed | tf_op | source)
XLA Modules:
  0.0 68.6 jit_solution(11342618965592503021)
XLA Ops:
  0.6 64.4 %shard_map.77 = (f32[8,2,2,16,256]{4,3,2,1,0:T(8,128)}, f32[8,2,16,256]{3,2,1,0:T(8,128)}) custom-call(bf16[8,2,2,16,256]{4,3,2,1,0:T(8,128)(2,1)} %bitcast.5, bf16[8,256,256]{2,1,0:T(8,128)(2,1)} %dinv_leaf.1, bf16[8,2,16,256]{3,2,1,0:T(8,128)(2,1)} %bitcast.7, bf16[8,256,256]{2,1,0:T(8,128)(2,1)} %dinv_sep.1, bf16[8,8,256,256]{3,2,1,0:T(8,128)(2,1)} %coupling.1, ...), custom_call_target="tpu_custom_call" | custom-call | tf_op jit(solution)/shard_map/pallas_call | solution.py:326
  65.1 1.9 %copy.10 = f32[8,64,256]{2,1,0:T(8,128)} copy(f32[8,64,256]{2,1,0:T(8,128)} %bitcast.4) | data formatting | bytes 1048576
  67.0 1.7 %copy.11 = f32[8,32,256]{2,1,0:T(8,128)} copy(f32[8,32,256]{2,1,0:T(8,128)} %bitcast.6) | data formatting | bytes 524288

commit v3 on v2

--- a/solution.py
+++ b/solution.py
@@ -10,7 +10,7 @@
 BF = jnp.bfloat16
 F32 = jnp.float32
 MESH = pl.DeviceIdType.MESH
-LAGS = (2, 5, 8, 10)
+LAGS = (2, 4, 6, 8)
 
 
 def factors(pc):
@@ -311,7 +311,7 @@
     nz, ny = factors(pc)
     ss, ls, bs, _ = coupling.shape
     g = pc // pr
-    nh = 2 if b_sep.shape[1] >= 16 else 1
+    nh = 1
     rs = b_sep.shape[1] // nh
     rl = g * rs
     step = 2

time: 68.8 us -> 66.2 us (0.962)
  Pallas kernels: 64.4 us -> 61.8 us
    pallas_call x1, Pallas kernels: 64.4 us -> 61.8 us  [shards(): pl.pallas_call(functools.partial(kernel, (nx, nz, ny, ls, ss, g, nh, rs,...]
where the time goes in v3:
time: 66.2 us; the launch traced here: 66 us
  Pallas kernels  61.8 us (93%)
  local copies, waits for them, and re-layouts  3.54 us (5%)
    pallas_call x1, Pallas kernels, shards(): pl.pallas_call(functools.partial(kernel, (nx, nz, ny, ls, ss, g, nh, rs,...  61.8 us
    unnamed x2, local copies, waits for them, and re-layouts  3.54 us

profile of v3, /device:TPU:0, one launch (start us, length us, event | category | flops | bytes accessed | tf_op | source)
XLA Modules:
  0.0 66.0 jit_solution(6495085844740873859)
XLA Ops:
  0.6 61.8 %shard_map.77 = (f32[8,2,1,32,256]{4,3,2,1,0:T(8,128)}, f32[8,1,32,256]{3,2,1,0:T(8,128)}) custom-call(bf16[8,2,1,32,256]{4,3,2,1,0:T(8,128)(2,1)} %bitcast.5, bf16[8,256,256]{2,1,0:T(8,128)(2,1)} %dinv_leaf.1, bf16[8,1,32,256]{3,2,1,0:T(8,128)(2,1)} %bitcast.7, bf16[8,256,256]{2,1,0:T(8,128)(2,1)} %dinv_sep.1, bf16[8,8,256,256]{3,2,1,0:T(8,128)(2,1)} %coupling.1, ...), custom_call_target="tpu_custom_call" | custom-call | tf_op jit(solution)/shard_map/pallas_call | solution.py:326
  62.4 1.9 %copy.10 = f32[8,64,256]{2,1,0:T(8,128)} copy(f32[8,64,256]{2,1,0:T(8,128)} %bitcast.4) | data formatting | bytes 1048576
  64.3 1.7 %copy.11 = f32[8,32,256]{2,1,0:T(8,128)} copy(f32[8,32,256]{2,1,0:T(8,128)} %bitcast.6) | data formatting | bytes 524288
